TPU v7x, 32 devices: a whole 2x2x4 slice. The times are simulated.
32 devices in a mesh: dp: 8 (over z, core), fsdp: 4 (over y, x).
Axes of the slice: x: 2, y: 2, z: 4, core: 2. Of those that a mesh axis runs over, the one named last changes fastest.
Arguments:
- inputs: bfloat16 [64, 512, 768], P(('dp', 'fsdp')), may hold values from -6 to 6
- segment_ids: int32 [64, 512], P(('dp', 'fsdp')), may hold values from 0 to 3, never falling along the last dimension, each value on 1 to 256 neighbouring positions
- cotangent: bfloat16 [64, 512, 768], P(('dp', 'fsdp')), may hold values from -9 to 9
- qkv_weight: bfloat16 [768, 2304], P(('dp', 'fsdp')), may hold values from -0.21875 to 0.21875
- out_weight: bfloat16 [768, 768], P(('dp', 'fsdp')), may hold values from -1.75 to 1.75
- up_weight: bfloat16 [768, 3072], P(('dp', 'fsdp')), may hold values from -0.21875 to 0.21875
- down_weight: bfloat16 [3072, 768], P(('dp', 'fsdp')), may hold values from -0.109375 to 0.109375
- query_bias_vector: bfloat16 [768], P(('dp', 'fsdp')), may hold values from -1.5 to 1.5
- value_bias_vector: bfloat16 [768], P(('dp', 'fsdp')), may hold values from -1.5 to 1.5
- out_bias: bfloat16 [768], P(('dp', 'fsdp')), may hold values from -1.5 to 1.5
- gain_one: bfloat16 [768], P(('dp', 'fsdp')), may hold values from 0.5 to 1.5
- shift_one: bfloat16 [768], P(('dp', 'fsdp')), may hold values from -1.5 to 1.5
- up_bias: bfloat16 [3072], P(('dp', 'fsdp')), may hold values from -1.5 to 1.5
- down_bias: bfloat16 [768], P(('dp', 'fsdp')), may hold values from -1.5 to 1.5
- gain_two: bfloat16 [768], P(('dp', 'fsdp')), may hold values from 0.5 to 1.5
- shift_two: bfloat16 [768], P(('dp', 'fsdp')), may hold values from -1.5 to 1.5
- query_down: bfloat16 [768, 8], replicated, may hold values from -0.21875 to 0.21875
- query_up_weight: bfloat16 [8, 768], replicated, may hold values from -2 to 2
- value_down: bfloat16 [768, 8], replicated, may hold values from -0.21875 to 0.21875
- value_up_weight: bfloat16 [8, 768], replicated, may hold values from -2 to 2
Outputs:
- output: bfloat16 [64, 512, 768], P(('dp', 'fsdp'))
- grad_input: float32 [64, 512, 768], P(('dp', 'fsdp'))
- grad_query_down: float32 [768, 8], replicated
- grad_query_up: float32 [8, 768], replicated
- grad_value_down: float32 [768, 8], replicated
- grad_value_up: float32 [8, 768], replicated
Inputs may be any that keep to these rules, and one draw needn't show every extreme that they name: `segment_ids`: within a pack the ids never fall; each of the 4 documents has 1 to 256 rows, and one has exactly 256.
All inputs are finite; a program needn't handle non-finite values.
Results may differ from a plain program's by a relative error of at most 0.015.
The roundings to bfloat16 on the way count: a program that leaves them out, or rounds other values in their place, can miss the bound.
Values may be sent and summed in bfloat16 or wider, within the bound.
No kernel may reach another device: no remote copies, remote signals or barrier semaphores. Data moves between devices by JAX's collectives and lax.ppermute only.
A program may use at most 128 MiB of HBM per device.

v0:
```python
from functools import partial
import jax
import jax.numpy as jnp
from jax import lax
from jax.sharding import PartitionSpec as P

HEADS = 12
HEAD_DIM = 64
highest_precision_mode = lax.Precision.HIGHEST
norm_epsilon = 1e-05
adapter_scale = 2.0


def layer_norm(value_rows, gain, shift):
    centred = value_rows - jnp.mean(value_rows, axis=-1, keepdims=True)
    variance = jnp.mean(centred * centred, axis=-1, keepdims=True)
    return centred * lax.rsqrt(variance + norm_epsilon) * gain + shift


def gelu_exact(value_rows):
    return jax.nn.gelu(value_rows, approximate=False)


def fetch_forward(qkv_weight, out_weight, up_weight, down_weight, vectors, up_bias):
    return (
        lax.all_gather(qkv_weight, ("dp", "fsdp"), axis=0, tiled=True),
        lax.all_gather(out_weight, ("dp", "fsdp"), axis=0, tiled=True),
        lax.all_gather(up_weight, ("dp", "fsdp"), axis=0, tiled=True),
        lax.all_gather(down_weight, ("dp", "fsdp"), axis=0, tiled=True),
        lax.all_gather(vectors, ("dp", "fsdp"), axis=1, tiled=True),
        lax.all_gather(up_bias, ("dp", "fsdp"), axis=0, tiled=True),
    )


def fetch_backward(qkv_weight, out_weight, up_weight, down_weight, gains):
    return (
        lax.all_gather(qkv_weight, ("dp", "fsdp"), axis=0, tiled=True),
        lax.all_gather(out_weight, ("dp", "fsdp"), axis=0, tiled=True),
        lax.all_gather(up_weight, ("dp", "fsdp"), axis=0, tiled=True),
        lax.all_gather(down_weight, ("dp", "fsdp"), axis=0, tiled=True),
        lax.all_gather(gains, ("dp", "fsdp"), axis=1, tiled=True),
    )


def segment_mask(segment):
    return (segment[:, None] == segment[None, :])[None]


def attend_pack(packed):
    query_rows, key_rows, value_rows, segment = packed
    scale = query_rows.shape[-1] ** (-0.5)
    raw_scores = jnp.einsum(
        "qhd,khd->hqk", query_rows, key_rows, preferred_element_type=jnp.float32
    )
    in_segment = segment_mask(segment)
    masked = jnp.where(in_segment, raw_scores * scale, -jnp.inf)
    highest = jnp.max(masked, axis=-1, keepdims=True)
    exponent = jnp.where(in_segment, jnp.exp(masked - highest), 0.0)
    row_total = jnp.sum(exponent, axis=-1, keepdims=True)
    probs_low = (exponent / row_total).astype(jnp.bfloat16)
    attended = jnp.einsum("hqk,khd->qhd", probs_low, value_rows, preferred_element_type=jnp.float32)
    return (attended, (highest + jnp.log(row_total))[..., 0])


def attend_back(packed):
    query_rows, key_rows, value_rows, segment, log_total, grad_mixed = packed
    scale = query_rows.shape[-1] ** (-0.5)
    raw_scores = jnp.einsum(
        "qhd,khd->hqk", query_rows, key_rows, preferred_element_type=jnp.float32
    )
    in_segment = segment_mask(segment)
    probs = jnp.where(in_segment, jnp.exp(raw_scores * scale - log_total[..., None]), 0.0)
    value_rows_gradient = jnp.einsum(
        "hqk,qhd->khd", probs.astype(jnp.bfloat16), grad_mixed, preferred_element_type=jnp.float32
    )
    grad_probs = jnp.einsum(
        "qhd,khd->hqk", grad_mixed, value_rows, preferred_element_type=jnp.float32
    )
    inner_sum = jnp.sum(probs * grad_probs, axis=-1, keepdims=True)
    grad_raw = (probs * (grad_probs - inner_sum) * scale).astype(jnp.bfloat16)
    query_rows_gradient = jnp.einsum(
        "hqk,khd->qhd", grad_raw, key_rows, preferred_element_type=jnp.float32
    )
    grad_keys = jnp.einsum("hqk,qhd->khd", grad_raw, query_rows, preferred_element_type=jnp.float32)
    return (
        query_rows_gradient.astype(jnp.bfloat16),
        grad_keys.astype(jnp.bfloat16),
        value_rows_gradient.astype(jnp.bfloat16),
    )


def local(
    inputs,
    segment_ids,
    cotangent,
    qkv_weight,
    out_weight,
    up_weight,
    down_weight,
    query_bias_vector,
    value_bias_vector,
    out_bias,
    gain_one,
    shift_one,
    up_bias,
    down_bias,
    gain_two,
    shift_two,
    query_down,
    query_up_weight,
    value_down,
    value_up_weight,
):
    vector_shards = jnp.stack(
        [
            query_bias_vector,
            value_bias_vector,
            out_bias,
            gain_one,
            shift_one,
            down_bias,
            gain_two,
            shift_two,
        ]
    )
    qkv_full, out_full, up_full, down_full, vector_full, up_bias_full = fetch_forward(
        qkv_weight, out_weight, up_weight, down_weight, vector_shards, up_bias
    )
    vectors = vector_full.astype(jnp.float32)
    packs, seq_len, width = inputs.shape
    rows = packs * seq_len
    flat_in = inputs.reshape(rows, width)
    flat_float = flat_in.astype(jnp.float32)
    projected_rows = jnp.dot(flat_in, qkv_full, preferred_element_type=jnp.float32)
    query_rank_rows = jnp.dot(flat_in, query_down, preferred_element_type=jnp.float32)
    value_rank_rows = jnp.dot(flat_in, value_down, preferred_element_type=jnp.float32)
    query_up_weight_float = query_up_weight.astype(jnp.float32)
    value_up_weight_float = value_up_weight.astype(jnp.float32)
    query_rows = (
        projected_rows[:, :width]
        + vectors[0]
        + adapter_scale
        * jnp.dot(query_rank_rows, query_up_weight_float, precision=highest_precision_mode)
    ).astype(jnp.bfloat16)
    key_rows = projected_rows[:, width : 2 * width].astype(jnp.bfloat16)
    value_rows = (
        projected_rows[:, 2 * width :]
        + vectors[1]
        + adapter_scale
        * jnp.dot(value_rank_rows, value_up_weight_float, precision=highest_precision_mode)
    ).astype(jnp.bfloat16)
    head_shape = (packs, seq_len, HEADS, HEAD_DIM)
    queries_heads = query_rows.reshape(head_shape)
    keys_heads = key_rows.reshape(head_shape)
    values_heads = value_rows.reshape(head_shape)
    attended, log_total = lax.map(
        attend_pack, (queries_heads, keys_heads, values_heads, segment_ids)
    )
    attended_low = attended.reshape(rows, width).astype(jnp.bfloat16)
    hidden_one = (
        flat_float
        + jnp.dot(attended_low, out_full, preferred_element_type=jnp.float32)
        + vectors[2]
    )
    normed_one = layer_norm(hidden_one, vectors[3], vectors[4])
    upper = jnp.dot(
        normed_one.astype(jnp.bfloat16), up_full, preferred_element_type=jnp.float32
    ) + up_bias_full.astype(jnp.float32)
    activated, gelu_pull = jax.vjp(gelu_exact, upper)
    hidden_two = (
        normed_one
        + jnp.dot(activated.astype(jnp.bfloat16), down_full, preferred_element_type=jnp.float32)
        + vectors[5]
    )
    output = layer_norm(hidden_two, vectors[6], vectors[7]).astype(jnp.bfloat16)
    gain_shards = jnp.stack([gain_one, gain_two])
    qkv_back, out_back, up_back, down_back, gain_back = fetch_backward(
        qkv_weight, out_weight, up_weight, down_weight, gain_shards
    )
    gain_back = gain_back.astype(jnp.float32)
    gain_back_one, gain_back_two = (gain_back[0], gain_back[1])
    grad_out = cotangent.reshape(rows, width).astype(jnp.float32)
    normed_again, pull_two = jax.vjp(partial(layer_norm, gain=gain_back_two, shift=0.0), hidden_two)
    (grad_two,) = pull_two(grad_out)
    grad_act = jnp.dot(
        grad_two.astype(jnp.bfloat16), down_back.T, preferred_element_type=jnp.float32
    )
    (grad_upper,) = gelu_pull(grad_act)
    grad_normed = grad_two + jnp.dot(
        grad_upper.astype(jnp.bfloat16), up_back.T, preferred_element_type=jnp.float32
    )
    first_again, pull_one = jax.vjp(partial(layer_norm, gain=gain_back_one, shift=0.0), hidden_one)
    (grad_one,) = pull_one(grad_normed)
    grad_mixed = jnp.dot(
        grad_one.astype(jnp.bfloat16), out_back.T, preferred_element_type=jnp.float32
    ).astype(jnp.bfloat16)
    query_rows_gradient, grad_keys, value_rows_gradient = lax.map(
        attend_back,
        (
            queries_heads,
            keys_heads,
            values_heads,
            segment_ids,
            log_total,
            grad_mixed.reshape(head_shape),
        ),
    )
    query_rows_gradient = query_rows_gradient.reshape(rows, width)
    value_rows_gradient = value_rows_gradient.reshape(rows, width)
    grad_project = jnp.concatenate(
        [query_rows_gradient, grad_keys.reshape(rows, width), value_rows_gradient], axis=1
    )
    query_rank_gradient = adapter_scale * jnp.dot(
        query_rows_gradient, query_up_weight.T, preferred_element_type=jnp.float32
    )
    value_rank_gradient = adapter_scale * jnp.dot(
        value_rows_gradient, value_up_weight.T, preferred_element_type=jnp.float32
    )
    grad_rows = grad_one + jnp.dot(grad_project, qkv_back.T, preferred_element_type=jnp.float32)
    grad_rows = grad_rows + jnp.dot(
        query_rank_gradient, query_down.astype(jnp.float32).T, precision=highest_precision_mode
    )
    grad_rows = grad_rows + jnp.dot(
        value_rank_gradient, value_down.astype(jnp.float32).T, precision=highest_precision_mode
    )
    term_query_up = jnp.dot(
        query_rank_rows.T,
        adapter_scale * query_rows_gradient.astype(jnp.float32),
        precision=highest_precision_mode,
    )
    term_value_up = jnp.dot(
        value_rank_rows.T,
        adapter_scale * value_rows_gradient.astype(jnp.float32),
        precision=highest_precision_mode,
    )
    term_query_down = jnp.dot(flat_float.T, query_rank_gradient, precision=highest_precision_mode)
    term_value_down = jnp.dot(flat_float.T, value_rank_gradient, precision=highest_precision_mode)
    sum_query_down, sum_query_up, sum_value_down, sum_value_up = lax.psum(
        (term_query_down, term_query_up, term_value_down, term_value_up), ("dp", "fsdp")
    )
    return (
        output.reshape(packs, seq_len, width),
        grad_rows.reshape(packs, seq_len, width),
        sum_query_down,
        sum_query_up,
        sum_value_down,
        sum_value_up,
    )


def solution(mesh):
    in_specs = (
        P(("dp", "fsdp"), None, None),
        P(("dp", "fsdp"), None),
        P(("dp", "fsdp"), None, None),
        P(("dp", "fsdp"), None),
        P(("dp", "fsdp"), None),
        P(("dp", "fsdp"), None),
        P(("dp", "fsdp"), None),
        P(("dp", "fsdp")),
        P(("dp", "fsdp")),
        P(("dp", "fsdp")),
        P(("dp", "fsdp")),
        P(("dp", "fsdp")),
        P(("dp", "fsdp")),
        P(("dp", "fsdp")),
        P(("dp", "fsdp")),
        P(("dp", "fsdp")),
        P(),
        P(),
        P(),
        P(),
    )
    out_specs = (P(("dp", "fsdp"), None, None), P(("dp", "fsdp"), None, None), P(), P(), P(), P())
    return jax.shard_map(local, mesh=mesh, in_specs=in_specs, out_specs=out_specs, check_vma=False)
```

profile of v0, /device:TPU:8, one launch (start us, length us, event | category | flops | bytes accessed | tf_op | source)
XLA Modules:
  0.0 645.6 jit_solution(10639014909072017310)
XLA Ops:
  11.6 57.1 %all-gather = bf16[32,24,8]{1,2,0:T(8,128)(2,1)S(1)} all-gather(bf16[1,24,8]{1,2,0:T(8,128)(2,1)S(1)} %bitcast.216), channel_id=1, replica_groups=mesh['dp'=8,'fsdp'=4] {'dp','fsdp'}, dimensions={0}, use_global_device_ids=true | all-gather | bytes 12672 | tf_op jit(solution)/shard_map/all_gather | solution.py:30
  73.8 50.2 %all-reduce = bf16[3072]{0:T(1024)(128)(2,1)S(1)} all-reduce(bf16[3072]{0:T(1024)(128)(2,1)S(1)} %dynamic-update-slice), channel_id=1, replica_groups=mesh['dp'=8,'fsdp'=4] {'dp','fsdp'}, use_global_device_ids=true, to_apply=%add | all-reduce | flops 3072 | bytes 12288
  124.7 51.4 %all-gather.1 = bf16[32,24,2]{1,2,0:T(2,128)(2,1)S(1)} all-gather(bf16[1,24,2]{1,2,0:T(2,128)(2,1)S(1)} %maximum_bitcast_fusion), channel_id=1, replica_groups=mesh['dp'=8,'fsdp'=4] {'dp','fsdp'}, dimensions={0}, use_global_device_ids=true | all-gather | bytes 3168 | tf_op jit(solution)/shard_map/all_gather | solution.py:41
  177.0 5.8 fusion.157
  183.0 3.4 copy-done.11
  196.6 4.6 fusion.120
  208.6 3.8 reshape.187
  214.2 23.0 %while.26 = (s32[]{:T(128)}, bf16[2,512,12,64]{1,3,2,0:T(8,128)(2,1)}, f32[2,12,512]{2,1,0:T(8,128)}, bf16[2,512,12,64]{1,3,2,0:T(8,128)(2,1)}, s32[2,512]{1,0:T...) while((s32[]{:T(128)}, ...), condition=%wide.region_3.4_spmd, body=%wide.region_0.3_spmd.sunk | while | flops 849602560 | bytes 49250932 | solution.py:156
  221.0 4.6 bitcast_dynamic-update-slice_fusion.4
  232.4 4.6 bitcast_dynamic-update-slice_fusion.4
  241.8 3.9 fusion.155
  248.0 36.6 %fusion.103 = (f32[1024,3072]{1,0:T(8,128)}, f32[1024,3072]{1,0:T(8,128)}) fusion(f32[3072]{0:T(1024)S(1)} %copy-done.29, bf16[768,3072]{1,0:T(8,128)(2,1)} %all-gather.11.cloned.1.call-done, f32[1024,768]{1,0:T(8,128)} %copy-done.7, f32[768]{0:T(1024)S(1)} %copy-done.31, f32[768]{0:T(1024)S(1)} %copy-done.32, f32[1024]{0:T(1024)S(1)} %fusion.144, ...), kind=kOutput, calls=%fused_computation.80 | convolution fusion | flops 5033951232 | bytes 33056768 | tf_op jit(solution)/shard_map/dot_general | solution.py:166
  284.6 16.2 %fusion.156 = (f32[1024]{0:T(1024)S(1)}, f32[1024,768]{1,0:T(8,128)S(1)}) fusion(f32[768]{0:T(1024)S(1)} %copy-done.30, bf16[3072,768]{1,0:T(8,128)(2,1)} %all-gather.13.cloned.1.call-done, f32[1024,3072]{1,0:T(8,128)} %get-tuple-element.232, f32[1024,3072]{1,0:T(8,128)} %get-tuple-element.233, f32[3072]{0:T(1024)S(1)} %copy-done.29, ...), kind=kOutput, calls=%fused_computation.183 | convolution fusion | flops 4849925120 | bytes 36209664 | tf_op jit(solution)/shard_map/dot_general | solution.py:172
  301.9 3.2 fusion.154
  305.2 23.1 %multiply_reduce_fusion.1 = (f32[1024]{0:T(1024)S(1)}, f32[1024,768]{1,0:T(8,128)}) fusion(f32[1024,768]{1,0:T(8,128)} %copy-done.7, f32[1024]{0:T(1024)S(1)} %broadcast_multiply_fusion.1, f32[768]{0:T(1024)S(1)} %copy-done.34, bf16[768,3072]{1,0:T(8,128)(2,1)} %all-gather.11.cloned.1.call-done, f32[1024,3072]{1,0:T(8,128)} %get-tuple-element.232, ...), kind=kOutput, calls=%fused_computation.126 | convolution fusion | flops 9717152768 | bytes 44067840 | tf_op jit(solution)/shard_map/dot_general | solution.py:189
  328.3 3.6 fusion.153
  338.9 3.8 reshape.189
  345.6 126.3 %while.27 = (s32[]{:T(128)}, bf16[2,512,12,64]{1,3,2,0:T(8,128)(2,1)}, bf16[2,512,12,64]{1,3,2,0:T(8,128)(2,1)}, bf16[2,512,12,64]{1,3,2,0:T(8,128)(2,1)}, bf16[...) while((s32[]{:T(128)}, ...), condition=%wide.region_14.15_spmd, body=%wide.region_12.14_spmd.sunk | while | flops 2096509952 | bytes 160648368 | solution.py:197
  345.8 6.4 fusion.229
  352.2 6.3 fusion.228
  360.2 20.3 %fusion.231 = bf16[2,512,12,64]{1,3,2,0:T(8,128)(2,1)} fusion(bf16[2,512,12,64]{1,3,2,0:T(8,128)(2,1)} %get-tuple-element.383, s32[]{:T(128)} %get-tuple-element.381, f32[12,512,512]{1,2,0:T(8,128)} %fusion.228, f32[12,512,512]{1,2,0:T(8,128)} %fusion.229, f32[12,512]{1,0:T(8,128)S(1)} %dynamic-slice_bitcast_fusion.2, ...), kind=kOutput, calls=%fused_computation.44.clone.1 | convolution fusion | flops 437656064 | bytes 52495360 | tf_op jit(solution)/shard_map/while/body/eval_jaxpr/hqk,qhd->khd/dot_general | solution.py:84
  380.5 20.1 %fusion.230 = bf16[2,512,12,64]{1,3,2,0:T(8,128)(2,1)} fusion(bf16[2,512,12,64]{1,3,2,0:T(8,128)(2,1)} %get-tuple-element.382, s32[]{:T(128)} %get-tuple-element.381, f32[12,512,512]{1,2,0:T(8,128)} %fusion.228, f32[12,512,512]{1,2,0:T(8,128)} %fusion.229, f32[12,512]{1,0:T(8,128)S(1)} %dynamic-slice_bitcast_fusion.2, ...), kind=kOutput, calls=%fused_computation.46.clone.1 | convolution fusion | flops 437656064 | bytes 52495360 | tf_op jit(solution)/shard_map/while/body/eval_jaxpr/hqk,khd->qhd/dot_general | solution.py:81
  400.6 8.3 %fusion.232 = bf16[2,512,12,64]{1,3,2,0:T(8,128)(2,1)} fusion(bf16[2,512,12,64]{1,3,2,0:T(8,128)(2,1)} %get-tuple-element.384, s32[]{:T(128)} %get-tuple-element.381, f32[12,512,512]{1,2,0:T(8,128)} %fusion.229, f32[12,512]{1,0:T(8,128)S(1)} %dynamic-slice_bitcast_fusion.2, pred[512,512]{0,1:T(8,128)(4,1)S(1)} %broadcast_compare_fusion.5, ...), kind=kOutput, calls=%fused_computation.48.clone.1 | convolution fusion | flops 415629312 | bytes 14443520 | tf_op jit(solution)/shard_map/while/body/eval_jaxpr/hqk,qhd->khd/dot_general | solution.py:73
  408.9 6.4 fusion.229
  415.3 6.3 fusion.228
  423.3 20.3 %fusion.231 = bf16[2,512,12,64]{1,3,2,0:T(8,128)(2,1)} fusion(bf16[2,512,12,64]{1,3,2,0:T(8,128)(2,1)} %get-tuple-element.383, s32[]{:T(128)} %get-tuple-element.381, f32[12,512,512]{1,2,0:T(8,128)} %fusion.228, f32[12,512,512]{1,2,0:T(8,128)} %fusion.229, f32[12,512]{1,0:T(8,128)S(1)} %dynamic-slice_bitcast_fusion.2, ...), kind=kOutput, calls=%fused_computation.44.clone.1 | convolution fusion | flops 437656064 | bytes 52495360 | tf_op jit(solution)/shard_map/while/body/eval_jaxpr/hqk,qhd->khd/dot_general | solution.py:84
  443.6 20.1 %fusion.230 = bf16[2,512,12,64]{1,3,2,0:T(8,128)(2,1)} fusion(bf16[2,512,12,64]{1,3,2,0:T(8,128)(2,1)} %get-tuple-element.382, s32[]{:T(128)} %get-tuple-element.381, f32[12,512,512]{1,2,0:T(8,128)} %fusion.228, f32[12,512,512]{1,2,0:T(8,128)} %fusion.229, f32[12,512]{1,0:T(8,128)S(1)} %dynamic-slice_bitcast_fusion.2, ...), kind=kOutput, calls=%fused_computation.46.clone.1 | convolution fusion | flops 437656064 | bytes 52495360 | tf_op jit(solution)/shard_map/while/body/eval_jaxpr/hqk,khd->qhd/dot_general | solution.py:81
  463.7 8.3 %fusion.232 = bf16[2,512,12,64]{1,3,2,0:T(8,128)(2,1)} fusion(bf16[2,512,12,64]{1,3,2,0:T(8,128)(2,1)} %get-tuple-element.384, s32[]{:T(128)} %get-tuple-element.381, f32[12,512,512]{1,2,0:T(8,128)} %fusion.229, f32[12,512]{1,0:T(8,128)S(1)} %dynamic-slice_bitcast_fusion.2, pred[512,512]{0,1:T(8,128)(4,1)S(1)} %broadcast_compare_fusion.5, ...), kind=kOutput, calls=%fused_computation.48.clone.1 | convolution fusion | flops 415629312 | bytes 14443520 | tf_op jit(solution)/shard_map/while/body/eval_jaxpr/hqk,qhd->khd/dot_general | solution.py:73
  495.9 3.1 copy.107
  500.7 6.6 %fusion.113 = f32[1024,768]{1,0:T(8,128)S(1)} fusion(bf16[768,2304]{1,0:T(8,128)(2,1)} %all-gather.7.cloned.1.call-done, bf16[1024,768]{0,1:T(8,128)(2,1)S(1)} %bitcast.200, bf16[1024,768]{0,1:T(8,128)(2,1)} %bitcast.210, bf16[1024,768]{0,1:T(8,128)(2,1)S(1)} %bitcast.203), kind=kOutput, calls=%fused_computation.102 | convolution fusion | flops 3638034432 | bytes 11403264 | tf_op jit(solution)/shard_map/dot_general | solution.py:219
  507.3 3.5 add_add_fusion.2
  510.8 122.5 %all-reduce.4.cloned.1.call-done = (f32[768,8]{0,1:T(8,128)}, f32[8,768]{1,0:T(8,128)}, f32[768,8]{0,1:T(8,128)}, f32[8,768]{1,0:T(8,128)}) async-done(((f32[768,8]{0,1:T(8,128)}, f32[8,768]{1,0:T(8,128)}, f32[768,8]{0,1:T(8,128)}, f32[8,768]{1,0:T(8,128)}), (f32[768,8]{0,1:T(8,128)}, f32[8,768]{1,0:T(8,128)}, f32[768,8]{0,1:T(8,128)}, f32[8,768]{1,0:T(8,128)})) %all-reduce.4.cloned.1.call-update) | async-done | bytes 98320 | tf_op jit(solution)/shard_map/psum | solution.py:238
  (171 shorter events, 95.8 us)
Async XLA Ops:
  7.2 179.3 %copy-start = (bf16[8,768]{1,0:T(8,128)(2,1)S(1)}, bf16[8,768]{1,0:T(8,128)(2,1)}, u32[]{:S(2)}) copy-start(bf16[8,768]{1,0:T(8,128)(2,1)} %param.43) | copy-start | bytes 36868
  7.2 169.8 %copy-start.1 = (bf16[2,512,768]{2,1,0:T(8,128)(2,1)S(1)}, bf16[2,512,768]{2,1,0:T(8,128)(2,1)}, u32[]{:S(2)}) copy-start(bf16[2,512,768]{2,1,0:T(8,128)(2,1)} %param.24) | copy-start | bytes 4718596
  7.2 66.4 %copy-start.36 = (bf16[96]{0:T(256)(128)(2,1)S(1)}, bf16[96]{0:T(256)(128)(2,1)}, u32[]{:S(2)}) copy-start(bf16[96]{0:T(256)(128)(2,1)} %param.36) | copy-start | bytes 580
  7.2 169.8 %all-gather.7.cloned.1.call-start = ((), (), s32[]{:S(2)}) async-start(), calls=%async_computation | async-start | bytes 3649536 | tf_op jit(solution)/shard_map/all_gather | solution.py:26
  7.9 233.8 %all-gather.9.cloned.1.call-start = ((), (), s32[]{:S(2)}) async-start(), calls=%async_computation.1 | async-start | bytes 1216512 | tf_op jit(solution)/shard_map/all_gather | solution.py:27
  8.7 239.2 %all-gather.11.cloned.1.call-start = ((), (), s32[]{:S(2)}) async-start(), calls=%async_computation.2 | async-start | bytes 4866048 | tf_op jit(solution)/shard_map/all_gather | solution.py:28
  9.4 275.1 %all-gather.13.cloned.1.call-start = ((), (), s32[]{:S(2)}) async-start(), calls=%async_computation.3 | async-start | bytes 4866048 | tf_op jit(solution)/shard_map/all_gather | solution.py:29
  10.0 623.3 %all-reduce.4.cloned.1.call-start = ((), (), s32[]{:S(2)}) async-start(), calls=%async_computation.4 | async-start | bytes 196608 | tf_op jit(solution)/shard_map/psum | solution.py:238
  71.6 111.4 %copy-start.18 = (f32[1024,8]{0,1:T(8,128)}, f32[1024,8]{0,1:T(8,128)S(1)}, u32[]{:S(2)}) copy-start(f32[1024,8]{0,1:T(8,128)S(1)} %fusion.158) | copy-start | bytes 98308
  73.5 123.0 %copy-start.16 = (f32[1024,8]{0,1:T(8,128)}, f32[1024,8]{0,1:T(8,128)S(1)}, u32[]{:S(2)}) copy-start(f32[1024,8]{0,1:T(8,128)S(1)} %fusion.159) | copy-start | bytes 98308
  191.3 5.3 copy-start.20
  237.1 4.6 copy-start.33
  247.9 36.6 %copy-start.30 = (f32[768]{0:T(1024)S(1)}, f32[768]{0:T(1024)}, u32[]{:S(2)}) copy-start(f32[768]{0:T(1024)} %get-tuple-element.175) | copy-start | bytes 9220
  284.6 16.3 %copy-start.12 = (bf16[2,512,768]{2,1,0:T(8,128)(2,1)S(1)}, bf16[2,512,768]{2,1,0:T(8,128)(2,1)}, u32[]{:S(2)}) copy-start(bf16[2,512,768]{2,1,0:T(8,128)(2,1)} %param.26) | copy-start | bytes 4718596
  284.6 16.3 %copy-start.24 = (f32[768]{0:T(1024)S(1)}, f32[768]{0:T(1024)}, u32[]{:S(2)}) copy-start(f32[768]{0:T(1024)} %get-tuple-element.182) | copy-start | bytes 9220
  328.3 5.3 copy-start.35
  345.8 6.4 copy-start.4
  345.8 6.4 copy-start.5
  408.9 6.4 copy-start.4
  408.9 6.4 copy-start.5
  478.9 4.5 copy-start.21
  480.6 4.8 copy-start.2
  480.6 6.1 copy-start.22
  483.5 6.3 copy-start.13
  483.5 6.3 copy-start.19
  485.4 6.8 %copy-start.14 = (bf16[1024,768]{1,0:T(8,128)(2,1)S(1)}, bf16[1024,768]{1,0:T(8,128)(2,1)}, u32[]{:S(2)}) copy-start(bf16[1024,768]{1,0:T(8,128)(2,1)} %copy.109) | copy-start | bytes 4718596
  485.4 6.8 %copy-start.17 = (f32[1024,8]{0,1:T(8,128)S(1)}, f32[1024,8]{0,1:T(8,128)}, u32[]{:S(2)}) copy-start(f32[1024,8]{0,1:T(8,128)} %copy-done.16) | copy-start | bytes 98308
  495.9 4.8 copy-start.6
  500.7 6.6 %copy-start.8 = (f32[1024,768]{1,0:T(8,128)S(1)}, f32[1024,768]{1,0:T(8,128)}, u32[]{:S(2)}) copy-start(f32[1024,768]{1,0:T(8,128)} %fusion.160) | copy-start | bytes 9437188
  500.7 6.6 %copy-start.10 = (f32[1024,768]{1,0:T(8,128)S(1)}, f32[1024,768]{1,0:T(8,128)}, u32[]{:S(2)}) copy-start(f32[1024,768]{1,0:T(8,128)} %copy-done.9) | copy-start | bytes 9437188
  500.7 6.6 %copy-start.23 = (bf16[768,8]{0,1:T(8,128)(2,1)S(1)}, bf16[768,8]{0,1:T(8,128)(2,1)}, u32[]{:S(2)}) copy-start(bf16[768,8]{0,1:T(8,128)(2,1)} %param.42) | copy-start | bytes 36868
  500.7 6.6 %copy-start.28 = (f32[1024]{0:T(1024)S(1)}, f32[1024]{0:T(1024)}, u32[]{:S(2)}) copy-start(f32[1024]{0:T(1024)} %copy-done.27) | copy-start | bytes 12292
  (13 other events, 30.4 us)
Sparse Core Ops, SparseCore 0:
  10.9 61.1 all-gather.6
  75.0 52.4 all-gather.8
  130.4 64.2 all-gather.10
  197.4 62.3 all-gather.12
  500.8 132.4 all-reduce.3
where the time goes:
time: 652 us; the launch traced here: 646 us
  matrix products  258 us (40%)
  blocking collectives  159 us (24%)
  waiting for transfers between devices  125 us (19%)
  local copies, waits for them, and re-layouts  70 us (11%)
  other arithmetic  18.1 us (3%)
  between operations  14.7 us (2%)
    psum x1, waiting for transfers between devices, local(): lax.psum((term_query_down, term_query_up, term_value_down, term_value_up)...  123 us
    all_gather x1, blocking collectives, fetch_forward(): lax.all_gather(vectors, ('dp', 'fsdp'), axis=1, tiled=True)  57.1 us
    all_gather x1, blocking collectives, fetch_backward(): lax.all_gather(gains, ('dp', 'fsdp'), axis=1, tiled=True)  51.4 us
    unnamed x1, blocking collectives  50.2 us
    dot_general x2, matrix products, attend_back(): jnp.einsum('hqk,qhd->khd', grad_raw, query_rows, preferred_element_type=j...  40.7 us
    dot_general x2, matrix products, attend_back(): jnp.einsum('hqk,khd->qhd', grad_raw, key_rows, preferred_element_type=jnp...  40.1 us
    dot_general x1, matrix products, local(): jnp.dot(normed_one.astype(jnp.bfloat16), up_full, preferred_element_type=...  36.6 us
    dot_general x1, matrix products, local(): jnp.dot(grad_upper.astype(jnp.bfloat16), up_back.T, preferred_element_typ...  23.1 us
  transfers between devices with their start and end apart: 5, of which 1 were waited for; matrix products, arithmetic and copies ran while one was open for 19% of the time, Pallas kernels for 0%

commit v1 on v0

--- a/solution.py
+++ b/solution.py
@@ -236,7 +236,7 @@
     term_query_down = jnp.dot(flat_float.T, query_rank_gradient, precision=highest_precision_mode)
     term_value_down = jnp.dot(flat_float.T, value_rank_gradient, precision=highest_precision_mode)
     sum_query_down, sum_query_up, sum_value_down, sum_value_up = lax.psum(
-        (term_query_down, term_query_up, term_value_down, term_value_up), ("dp", "fsdp")
+        lax.psum((term_query_down, term_query_up, term_value_down, term_value_up), "fsdp"), "dp"
     )
     return (
         output.reshape(packs, seq_len, width),

time: 652 us -> 622 us (0.954)
  waiting for transfers between devices: 125 us -> 93.8 us
    psum x1, waiting for transfers between devices: 123 us -> 41.6 us  [local(): lax.psum((term_query_down, term_query_up, term_value_down, term_value_up)...]
    psum x0 -> x1, waiting for transfers between devices: none -> 49.6 us  [local(): lax.psum(lax.psum((term_query_down, term_query_up, term_value_down, term_...]
    unnamed x78 -> x70, local copies, waits for them, and re-layouts: 17.8 us -> 16.6 us
  transfers between devices with their start and end apart: 5 -> 6, of which waited for: 1 -> 2; matrix products, arithmetic and copies ran while one was open for 19% -> 20% of each run, Pallas kernels for 0% -> 0%
where the time goes in v1:
time: 622 us; the launch traced here: 615 us
  matrix products  261 us (42%)
  blocking collectives  159 us (26%)
  waiting for transfers between devices  93.8 us (15%)
  local copies, waits for them, and re-layouts  67.2 us (11%)
  other arithmetic  18.1 us (3%)
  between operations  14.8 us (2%)
    all_gather x1, blocking collectives, fetch_forward(): lax.all_gather(vectors, ('dp', 'fsdp'), axis=1, tiled=True)  57.1 us
    all_gather x1, blocking collectives, fetch_backward(): lax.all_gather(gains, ('dp', 'fsdp'), axis=1, tiled=True)  51.5 us
    unnamed x1, blocking collectives  50.2 us
    psum x1, waiting for transfers between devices, local(): lax.psum(lax.psum((term_query_down, term_query_up, term_value_down, term_...  49.6 us
    psum x1, waiting for transfers between devices, local(): lax.psum((term_query_down, term_query_up, term_value_down, term_value_up)...  41.6 us
    dot_general x2, matrix products, attend_back(): jnp.einsum('hqk,qhd->khd', grad_raw, query_rows, preferred_element_type=j...  40.7 us
    dot_general x2, matrix products, attend_back(): jnp.einsum('hqk,khd->qhd', grad_raw, key_rows, preferred_element_type=jnp...  40.1 us
    dot_general x1, matrix products, local(): jnp.dot(normed_one.astype(jnp.bfloat16), up_full, preferred_element_type=...  36.6 us
  transfers between devices with their start and end apart: 6, of which 2 were waited for; matrix products, arithmetic and copies ran while one was open for 20% of the time, Pallas kernels for 0%

profile of v1, /device:TPU:8, one launch (start us, length us, event | category | flops | bytes accessed | tf_op | source)
XLA Modules:
  0.0 615.3 jit_solution(17712288179426306586)
XLA Ops:
  11.6 57.1 %all-gather = bf16[32,24,8]{1,2,0:T(8,128)(2,1)S(1)} all-gather(bf16[1,24,8]{1,2,0:T(8,128)(2,1)S(1)} %bitcast.216), channel_id=1, replica_groups=mesh['dp'=8,'fsdp'=4] {'dp','fsdp'}, dimensions={0}, use_global_device_ids=true | all-gather | bytes 12672 | tf_op jit(solution)/shard_map/all_gather | solution.py:30
  73.8 50.2 %all-reduce = bf16[3072]{0:T(1024)(128)(2,1)S(1)} all-reduce(bf16[3072]{0:T(1024)(128)(2,1)S(1)} %dynamic-update-slice), channel_id=1, replica_groups=mesh['dp'=8,'fsdp'=4] {'dp','fsdp'}, use_global_device_ids=true, to_apply=%add | all-reduce | flops 3072 | bytes 12288
  124.6 51.5 %all-gather.1 = bf16[32,24,2]{1,2,0:T(2,128)(2,1)S(1)} all-gather(bf16[1,24,2]{1,2,0:T(2,128)(2,1)S(1)} %maximum_bitcast_fusion), channel_id=1, replica_groups=mesh['dp'=8,'fsdp'=4] {'dp','fsdp'}, dimensions={0}, use_global_device_ids=true | all-gather | bytes 3168 | tf_op jit(solution)/shard_map/all_gather | solution.py:41
  177.0 5.8 fusion.157
  183.0 3.4 copy-done.8
  196.4 4.6 fusion.120
  208.5 3.8 reshape.187
  214.0 23.3 %while.26 = (s32[]{:T(128)}, bf16[2,512,12,64]{1,3,2,0:T(8,128)(2,1)}, f32[2,12,512]{2,1,0:T(8,128)}, bf16[2,512,12,64]{1,3,2,0:T(8,128)(2,1)}, s32[2,512]{1,0:T...) while((s32[]{:T(128)}, ...), condition=%wide.region_3.4_spmd, body=%wide.region_0.3_spmd.sunk | while | flops 849602560 | bytes 49250932 | solution.py:156
  220.8 4.6 bitcast_dynamic-update-slice_fusion.4
  232.2 4.6 bitcast_dynamic-update-slice_fusion.4
  242.0 3.9 fusion.155
  248.2 36.6 %fusion.103 = (f32[1024,3072]{1,0:T(8,128)}, f32[1024,3072]{1,0:T(8,128)}) fusion(f32[3072]{0:T(1024)S(1)} %copy-done.25, bf16[768,3072]{1,0:T(8,128)(2,1)} %all-gather.11.cloned.1.call-done, f32[1024,768]{1,0:T(8,128)} %copy-done.6, f32[768]{0:T(1024)S(1)} %copy-done.27, f32[768]{0:T(1024)S(1)} %copy-done.28, f32[1024]{0:T(1024)S(1)} %fusion.144, ...), kind=kOutput, calls=%fused_computation.80 | convolution fusion | flops 5033951232 | bytes 33056768 | tf_op jit(solution)/shard_map/dot_general | solution.py:166
  284.8 16.0 %fusion.156 = (f32[1024]{0:T(1024)S(1)}, f32[1024,768]{1,0:T(8,128)S(1)}) fusion(f32[768]{0:T(1024)S(1)} %copy-done.26, bf16[3072,768]{1,0:T(8,128)(2,1)} %all-gather.13.cloned.1.call-done, f32[1024,3072]{1,0:T(8,128)} %get-tuple-element.236, f32[1024,3072]{1,0:T(8,128)} %get-tuple-element.237, f32[3072]{0:T(1024)S(1)} %copy-done.25, ...), kind=kOutput, calls=%fused_computation.183 | convolution fusion | flops 4849925120 | bytes 36209664 | tf_op jit(solution)/shard_map/dot_general | solution.py:172
  305.2 23.1 %multiply_reduce_fusion.1 = (f32[1024]{0:T(1024)S(1)}, f32[1024,768]{1,0:T(8,128)}) fusion(f32[1024,768]{1,0:T(8,128)} %copy-done.6, f32[1024]{0:T(1024)S(1)} %broadcast_multiply_fusion.1, f32[768]{0:T(1024)S(1)} %copy-done.30, bf16[768,3072]{1,0:T(8,128)(2,1)} %all-gather.11.cloned.1.call-done, f32[1024,3072]{1,0:T(8,128)} %get-tuple-element.236, ...), kind=kOutput, calls=%fused_computation.126 | convolution fusion | flops 9717152768 | bytes 44067840 | tf_op jit(solution)/shard_map/dot_general | solution.py:189
  328.4 3.6 fusion.153
  338.9 3.8 reshape.189
  345.6 126.8 %while.27 = (s32[]{:T(128)}, bf16[2,512,12,64]{1,3,2,0:T(8,128)(2,1)}, bf16[2,512,12,64]{1,3,2,0:T(8,128)(2,1)}, bf16[2,512,12,64]{1,3,2,0:T(8,128)(2,1)}, bf16[...) while((s32[]{:T(128)}, ...), condition=%wide.region_14.15_spmd, body=%wide.region_12.14_spmd.sunk | while | flops 2096509952 | bytes 160648368 | solution.py:197
  345.9 6.4 %fusion.229 = f32[12,512,512]{1,2,0:T(8,128)} fusion(bf16[2,512,12,64]{1,3,2,0:T(8,128)(2,1)S(1)} %get-tuple-element.402, s32[]{:T(128)} %get-tuple-element.385, bf16[2,512,12,64]{1,3,2,0:T(8,128)(2,1)S(1)} %get-tuple-element.400), kind=kOutput, calls=%fused_computation.54.clone.1 | convolution fusion | flops 402653184 | bytes 14156800 | tf_op jit(solution)/shard_map/while/body/eval_jaxpr/qhd,khd->hqk/dot_general | solution.py:68
  352.3 6.3 %fusion.228 = f32[12,512,512]{1,2,0:T(8,128)} fusion(bf16[2,512,12,64]{1,3,2,0:T(8,128)(2,1)S(1)} %copy-done.4, s32[]{:T(128)} %get-tuple-element.385, bf16[2,512,12,64]{1,3,2,0:T(8,128)(2,1)S(1)} %copy-done.5), kind=kOutput, calls=%fused_computation.49.clone.1 | convolution fusion | flops 402653184 | bytes 14156800 | tf_op jit(solution)/shard_map/while/body/eval_jaxpr/qhd,khd->hqk/dot_general | solution.py:76
  360.3 20.3 %fusion.231 = bf16[2,512,12,64]{1,3,2,0:T(8,128)(2,1)} fusion(bf16[2,512,12,64]{1,3,2,0:T(8,128)(2,1)} %get-tuple-element.387, s32[]{:T(128)} %get-tuple-element.385, f32[12,512,512]{1,2,0:T(8,128)} %fusion.228, f32[12,512,512]{1,2,0:T(8,128)} %fusion.229, f32[12,512]{1,0:T(8,128)S(1)} %dynamic-slice_bitcast_fusion.2, ...), kind=kOutput, calls=%fused_computation.44.clone.1 | convolution fusion | flops 437656064 | bytes 52495360 | tf_op jit(solution)/shard_map/while/body/eval_jaxpr/hqk,qhd->khd/dot_general | solution.py:84
  380.6 20.1 %fusion.230 = bf16[2,512,12,64]{1,3,2,0:T(8,128)(2,1)} fusion(bf16[2,512,12,64]{1,3,2,0:T(8,128)(2,1)} %get-tuple-element.386, s32[]{:T(128)} %get-tuple-element.385, f32[12,512,512]{1,2,0:T(8,128)} %fusion.228, f32[12,512,512]{1,2,0:T(8,128)} %fusion.229, f32[12,512]{1,0:T(8,128)S(1)} %dynamic-slice_bitcast_fusion.2, ...), kind=kOutput, calls=%fused_computation.46.clone.1 | convolution fusion | flops 437656064 | bytes 52495360 | tf_op jit(solution)/shard_map/while/body/eval_jaxpr/hqk,khd->qhd/dot_general | solution.py:81
  400.7 8.3 %fusion.232 = bf16[2,512,12,64]{1,3,2,0:T(8,128)(2,1)} fusion(bf16[2,512,12,64]{1,3,2,0:T(8,128)(2,1)} %get-tuple-element.388, s32[]{:T(128)} %get-tuple-element.385, f32[12,512,512]{1,2,0:T(8,128)} %fusion.229, f32[12,512]{1,0:T(8,128)S(1)} %dynamic-slice_bitcast_fusion.2, pred[512,512]{0,1:T(8,128)(4,1)S(1)} %broadcast_compare_fusion.5, ...), kind=kOutput, calls=%fused_computation.48.clone.1 | convolution fusion | flops 415629312 | bytes 14443520 | tf_op jit(solution)/shard_map/while/body/eval_jaxpr/hqk,qhd->khd/dot_general | solution.py:73
  409.0 6.4 %fusion.229 = f32[12,512,512]{1,2,0:T(8,128)} fusion(bf16[2,512,12,64]{1,3,2,0:T(8,128)(2,1)S(1)} %get-tuple-element.402, s32[]{:T(128)} %get-tuple-element.385, bf16[2,512,12,64]{1,3,2,0:T(8,128)(2,1)S(1)} %get-tuple-element.400), kind=kOutput, calls=%fused_computation.54.clone.1 | convolution fusion | flops 402653184 | bytes 14156800 | tf_op jit(solution)/shard_map/while/body/eval_jaxpr/qhd,khd->hqk/dot_general | solution.py:68
  415.4 6.3 %fusion.228 = f32[12,512,512]{1,2,0:T(8,128)} fusion(bf16[2,512,12,64]{1,3,2,0:T(8,128)(2,1)S(1)} %copy-done.4, s32[]{:T(128)} %get-tuple-element.385, bf16[2,512,12,64]{1,3,2,0:T(8,128)(2,1)S(1)} %copy-done.5), kind=kOutput, calls=%fused_computation.49.clone.1 | convolution fusion | flops 402653184 | bytes 14156800 | tf_op jit(solution)/shard_map/while/body/eval_jaxpr/qhd,khd->hqk/dot_general | solution.py:76
  423.4 20.3 %fusion.231 = bf16[2,512,12,64]{1,3,2,0:T(8,128)(2,1)} fusion(bf16[2,512,12,64]{1,3,2,0:T(8,128)(2,1)} %get-tuple-element.387, s32[]{:T(128)} %get-tuple-element.385, f32[12,512,512]{1,2,0:T(8,128)} %fusion.228, f32[12,512,512]{1,2,0:T(8,128)} %fusion.229, f32[12,512]{1,0:T(8,128)S(1)} %dynamic-slice_bitcast_fusion.2, ...), kind=kOutput, calls=%fused_computation.44.clone.1 | convolution fusion | flops 437656064 | bytes 52495360 | tf_op jit(solution)/shard_map/while/body/eval_jaxpr/hqk,qhd->khd/dot_general | solution.py:84
  443.7 20.1 %fusion.230 = bf16[2,512,12,64]{1,3,2,0:T(8,128)(2,1)} fusion(bf16[2,512,12,64]{1,3,2,0:T(8,128)(2,1)} %get-tuple-element.386, s32[]{:T(128)} %get-tuple-element.385, f32[12,512,512]{1,2,0:T(8,128)} %fusion.228, f32[12,512,512]{1,2,0:T(8,128)} %fusion.229, f32[12,512]{1,0:T(8,128)S(1)} %dynamic-slice_bitcast_fusion.2, ...), kind=kOutput, calls=%fused_computation.46.clone.1 | convolution fusion | flops 437656064 | bytes 52495360 | tf_op jit(solution)/shard_map/while/body/eval_jaxpr/hqk,khd->qhd/dot_general | solution.py:81
  463.7 8.3 %fusion.232 = bf16[2,512,12,64]{1,3,2,0:T(8,128)(2,1)} fusion(bf16[2,512,12,64]{1,3,2,0:T(8,128)(2,1)} %get-tuple-element.388, s32[]{:T(128)} %get-tuple-element.385, f32[12,512,512]{1,2,0:T(8,128)} %fusion.229, f32[12,512]{1,0:T(8,128)S(1)} %dynamic-slice_bitcast_fusion.2, pred[512,512]{0,1:T(8,128)(4,1)S(1)} %broadcast_compare_fusion.5, ...), kind=kOutput, calls=%fused_computation.48.clone.1 | convolution fusion | flops 415629312 | bytes 14443520 | tf_op jit(solution)/shard_map/while/body/eval_jaxpr/hqk,qhd->khd/dot_general | solution.py:73
  481.8 3.9 fusion.126
  495.6 8.1 %fusion.113 = f32[1024,768]{1,0:T(8,128)} fusion(bf16[768,2304]{1,0:T(8,128)(2,1)} %all-gather.7.cloned.1.call-done, bf16[1024,768]{0,1:T(8,128)(2,1)S(1)} %bitcast.200, bf16[1024,768]{0,1:T(8,128)(2,1)} %bitcast.210, bf16[1024,768]{0,1:T(8,128)(2,1)S(1)} %bitcast.203), kind=kOutput, calls=%fused_computation.102 | convolution fusion | flops 3638034432 | bytes 11403264 | tf_op jit(solution)/shard_map/dot_general | solution.py:219
  505.2 41.6 %all-reduce.8.cloned.1.call-done = (f32[768,8]{0,1:T(8,128)}, f32[8,768]{1,0:T(8,128)}, f32[768,8]{0,1:T(8,128)}, f32[8,768]{1,0:T(8,128)}) async-done(((f32[768,8]{0,1:T(8,128)}, f32[8,768]{1,0:T(8,128)}, f32[768,8]{0,1:T(8,128)}, f32[8,768]{1,0:T(8,128)}), (f32[768,8]{0,1:T(8,128)}, f32[8,768]{1,0:T(8,128)}, f32[768,8]{0,1:T(8,128)}, f32[8,768]{1,0:T(8,128)})) %all-reduce.8.cloned.1.call-update) | async-done | bytes 98320 | tf_op jit(solution)/shard_map/psum | solution.py:239
  546.8 6.5 %add_add_fusion.2 = f32[1024,768]{1,0:T(8,128)} fusion(f32[1024,768]{1,0:T(8,128)S(1)} %fusion.160, f32[1024,768]{1,0:T(8,128)} %fusion.113, f32[1024,768]{1,0:T(8,128)} %copy-done.7, f32[1024,8]{0,1:T(8,128)S(1)} %convolution_multiply_fusion, bf16[768,8]{0,1:T(8,128)(2,1)S(1)} %copy-done.19, f32[1024]{0:T(1024)S(1)} %copy-done.24), kind=kOutput, calls=%fused_computation.125 | convolution fusion | flops 78643200 | bytes 12632064 | tf_op jit(solution)/shard_map/dot_general | solution.py:223
  553.3 49.6 %all-reduce.6.cloned.1.call-done = (f32[768,8]{0,1:T(8,128)}, f32[8,768]{1,0:T(8,128)}, f32[768,8]{0,1:T(8,128)}, f32[8,768]{1,0:T(8,128)}) async-done(((f32[768,8]{0,1:T(8,128)}, f32[8,768]{1,0:T(8,128)}, f32[768,8]{0,1:T(8,128)}, f32[8,768]{1,0:T(8,128)}), (f32[768,8]{0,1:T(8,128)}, f32[8,768]{1,0:T(8,128)}, f32[768,8]{0,1:T(8,128)}, f32[8,768]{1,0:T(8,128)})) %all-reduce.6.cloned.1.call-update) | async-done | bytes 98320 | tf_op jit(solution)/shard_map/psum | solution.py:238
  (166 shorter events, 94.1 us)
Async XLA Ops:
  7.2 179.3 %copy-start = (bf16[8,768]{1,0:T(8,128)(2,1)S(1)}, bf16[8,768]{1,0:T(8,128)(2,1)}, u32[]{:S(2)}) copy-start(bf16[8,768]{1,0:T(8,128)(2,1)} %param.43) | copy-start | bytes 36868
  7.2 169.8 %copy-start.1 = (bf16[2,512,768]{2,1,0:T(8,128)(2,1)S(1)}, bf16[2,512,768]{2,1,0:T(8,128)(2,1)}, u32[]{:S(2)}) copy-start(bf16[2,512,768]{2,1,0:T(8,128)(2,1)} %param.24) | copy-start | bytes 4718596
  7.2 66.4 %copy-start.32 = (bf16[96]{0:T(256)(128)(2,1)S(1)}, bf16[96]{0:T(256)(128)(2,1)}, u32[]{:S(2)}) copy-start(bf16[96]{0:T(256)(128)(2,1)} %param.36) | copy-start | bytes 580
  7.2 169.8 %all-gather.7.cloned.1.call-start = ((), (), s32[]{:S(2)}) async-start(), calls=%async_computation | async-start | bytes 3649536 | tf_op jit(solution)/shard_map/all_gather | solution.py:26
  7.9 234.0 %all-gather.9.cloned.1.call-start = ((), (), s32[]{:S(2)}) async-start(), calls=%async_computation.1 | async-start | bytes 1216512 | tf_op jit(solution)/shard_map/all_gather | solution.py:27
  8.7 239.4 %all-gather.11.cloned.1.call-start = ((), (), s32[]{:S(2)}) async-start(), calls=%async_computation.2 | async-start | bytes 4866048 | tf_op jit(solution)/shard_map/all_gather | solution.py:28
  9.4 275.3 %all-gather.13.cloned.1.call-start = ((), (), s32[]{:S(2)}) async-start(), calls=%async_computation.3 | async-start | bytes 4866048 | tf_op jit(solution)/shard_map/all_gather | solution.py:29
  10.0 536.8 %all-reduce.8.cloned.1.call-start = ((), (), s32[]{:S(2)}) async-start(), calls=%async_computation.5 | async-start | bytes 196608 | tf_op jit(solution)/shard_map/psum | solution.py:239
  71.6 111.4 %copy-start.14 = (f32[1024,8]{0,1:T(8,128)}, f32[1024,8]{0,1:T(8,128)S(1)}, u32[]{:S(2)}) copy-start(f32[1024,8]{0,1:T(8,128)S(1)} %fusion.158) | copy-start | bytes 98308
  73.5 122.9 %copy-start.12 = (f32[1024,8]{0,1:T(8,128)}, f32[1024,8]{0,1:T(8,128)S(1)}, u32[]{:S(2)}) copy-start(f32[1024,8]{0,1:T(8,128)S(1)} %fusion.159) | copy-start | bytes 98308
  182.9 3.6 copy-start.8
  191.2 5.3 copy-start.16
  217.1 3.8 copy-start.3
  228.5 3.8 copy-start.3
  237.4 4.6 copy-start.29
  245.9 2.2 copy-start.25
  248.2 36.6 %copy-start.26 = (f32[768]{0:T(1024)S(1)}, f32[768]{0:T(1024)}, u32[]{:S(2)}) copy-start(f32[768]{0:T(1024)} %get-tuple-element.175) | copy-start | bytes 9220
  284.8 16.1 %copy-start.9 = (bf16[2,512,768]{2,1,0:T(8,128)(2,1)S(1)}, bf16[2,512,768]{2,1,0:T(8,128)(2,1)}, u32[]{:S(2)}) copy-start(bf16[2,512,768]{2,1,0:T(8,128)(2,1)} %param.26) | copy-start | bytes 4718596
  284.8 16.1 %copy-start.20 = (f32[768]{0:T(1024)S(1)}, f32[768]{0:T(1024)}, u32[]{:S(2)}) copy-start(f32[768]{0:T(1024)} %get-tuple-element.182) | copy-start | bytes 9220
  302.0 3.3 copy-start.30
  328.3 5.3 copy-start.31
  345.8 6.4 %copy-start.4 = (bf16[2,512,12,64]{1,3,2,0:T(8,128)(2,1)S(1)}, bf16[2,512,12,64]{1,3,2,0:T(8,128)(2,1)}, u32[]{:S(2)}) copy-start(bf16[2,512,12,64]{1,3,2,0:T(8,128)(2,1)} %get-tuple-element.405) | copy-start | bytes 4718596 | tf_op jit(solution)/shard_map/while
  345.9 6.4 %copy-start.5 = (bf16[2,512,12,64]{1,3,2,0:T(8,128)(2,1)S(1)}, bf16[2,512,12,64]{1,3,2,0:T(8,128)(2,1)}, u32[]{:S(2)}) copy-start(bf16[2,512,12,64]{1,3,2,0:T(8,128)(2,1)} %get-tuple-element.404) | copy-start | bytes 4718596 | tf_op jit(solution)/shard_map/while
  409.0 6.4 %copy-start.4 = (bf16[2,512,12,64]{1,3,2,0:T(8,128)(2,1)S(1)}, bf16[2,512,12,64]{1,3,2,0:T(8,128)(2,1)}, u32[]{:S(2)}) copy-start(bf16[2,512,12,64]{1,3,2,0:T(8,128)(2,1)} %get-tuple-element.405) | copy-start | bytes 4718596 | tf_op jit(solution)/shard_map/while
  409.0 6.4 %copy-start.5 = (bf16[2,512,12,64]{1,3,2,0:T(8,128)(2,1)S(1)}, bf16[2,512,12,64]{1,3,2,0:T(8,128)(2,1)}, u32[]{:S(2)}) copy-start(bf16[2,512,12,64]{1,3,2,0:T(8,128)(2,1)} %get-tuple-element.404) | copy-start | bytes 4718596 | tf_op jit(solution)/shard_map/while
  479.8 5.8 copy-start.13
  481.4 4.3 copy-start.10
  481.4 6.6 %copy-start.2 = (bf16[2,512,768]{2,1,0:T(8,128)(2,1)S(1)}, bf16[2,512,768]{2,1,0:T(8,128)(2,1)}, u32[]{:S(2)}) copy-start(bf16[2,512,768]{2,1,0:T(8,128)(2,1)} %param.24) | copy-start | bytes 4718596
  495.4 107.5 %all-reduce.6.cloned.1.call-start = ((), (), s32[]{:S(2)}) async-start(), calls=%async_computation.4 | async-start | bytes 196608 | tf_op jit(solution)/shard_map/psum | solution.py:238
  495.6 8.1 %copy-start.18 = (bf16[768,8]{0,1:T(8,128)(2,1)S(1)}, bf16[768,8]{0,1:T(8,128)(2,1)}, u32[]{:S(2)}) copy-start(bf16[768,8]{0,1:T(8,128)(2,1)} %param.40) | copy-start | bytes 36868
  503.7 43.1 %copy-start.19 = (bf16[768,8]{0,1:T(8,128)(2,1)S(1)}, bf16[768,8]{0,1:T(8,128)(2,1)}, u32[]{:S(2)}) copy-start(bf16[768,8]{0,1:T(8,128)(2,1)} %param.42) | copy-start | bytes 36868
  503.7 43.1 %copy-start.24 = (f32[1024]{0:T(1024)S(1)}, f32[1024]{0:T(1024)}, u32[]{:S(2)}) copy-start(f32[1024]{0:T(1024)} %copy-done.23) | copy-start | bytes 12292
  (10 other events, 17.7 us)
Sparse Core Ops, SparseCore 0:
  10.9 61.1 all-gather.6
  75.0 52.4 all-gather.8
  130.4 64.2 all-gather.10
  197.4 62.3 all-gather.12
  495.5 51.2 all-reduce.7
  549.4 53.4 all-reduce.5
